TPU v7x, 32 devices: a whole 2x2x4 slice. The times are simulated.
32 devices in a mesh: fsdp: 8 (over y, x, core), dp: 4 (over z).
Axes of the slice: x: 2, y: 2, z: 4, core: 2. Of those that a mesh axis runs over, the one named last changes fastest.
Arguments:
- hidden_in: bfloat16 [17408, 1024], P(('fsdp', 'dp')), may hold values from -6 to 6
- cotangent: bfloat16 [17408, 1024], P(('fsdp', 'dp')), may hold values from -6 to 6
- segment_ids: int32 [32, 544], P(('fsdp', 'dp')), may hold values from 0 to 7, never falling along the last dimension, each value on 1 to 128 neighbouring positions
- box_left: int32 [32, 544], P(('fsdp', 'dp')), may hold values from 0 to 63
- box_top: int32 [32, 544], P(('fsdp', 'dp')), may hold values from 0 to 63
- query_weight: bfloat16 [1024, 1024], P('fsdp'), may hold values from -0.1875 to 0.1875
- query_bias: bfloat16 [1024], P('fsdp'), may hold values from -3 to 3
- key_weight: bfloat16 [1024, 1024], P('fsdp'), may hold values from -0.1875 to 0.1875
- value_weight: bfloat16 [1024, 1024], P('fsdp'), may hold values from -0.1875 to 0.1875
- value_bias: bfloat16 [1024], P('fsdp'), may hold values from -3 to 3
- output_weight: bfloat16 [1024, 1024], P('fsdp'), may hold values from -0.75 to 0.75
- output_bias: bfloat16 [1024], P('fsdp'), may hold values from -2 to 2
- first_gain: bfloat16 [1024], P('fsdp'), may hold values from 0.25 to 1.75
- first_shift: bfloat16 [1024], P('fsdp'), may hold values from -2 to 2
- inner_weight: bfloat16 [1024, 4096], P('fsdp'), may hold values from -0.1875 to 0.1875
- inner_bias: bfloat16 [4096], P('fsdp'), may hold values from -3 to 3
- outer_weight: bfloat16 [4096, 1024], P('fsdp'), may hold values from -0.125 to 0.125
- outer_bias: bfloat16 [1024], P('fsdp'), may hold values from -2 to 2
- second_gain: bfloat16 [1024], P('fsdp'), may hold values from 0.25 to 1.75
- second_shift: bfloat16 [1024], P('fsdp'), may hold values from -2 to 2
- bucket_table: bfloat16 [6144], P('fsdp'), may hold values from -5 to 5
Outputs:
- layer_out: bfloat16 [17408, 1024], P(('fsdp', 'dp'))
- input_grad: float32 [17408, 1024], P(('fsdp', 'dp'))
- query_weight_grad: float32 [1024, 1024], P('fsdp')
- query_bias_grad: float32 [1024], P('fsdp')
- key_weight_grad: float32 [1024, 1024], P('fsdp')
- value_weight_grad: float32 [1024, 1024], P('fsdp')
- value_bias_grad: float32 [1024], P('fsdp')
- output_weight_grad: float32 [1024, 1024], P('fsdp')
- output_bias_grad: float32 [1024], P('fsdp')
- first_gain_grad: float32 [1024], P('fsdp')
- first_shift_grad: float32 [1024], P('fsdp')
- inner_weight_grad: float32 [1024, 4096], P('fsdp')
- inner_bias_grad: float32 [4096], P('fsdp')
- outer_weight_grad: float32 [4096, 1024], P('fsdp')
- outer_bias_grad: float32 [1024], P('fsdp')
- second_gain_grad: float32 [1024], P('fsdp')
- second_shift_grad: float32 [1024], P('fsdp')
- bucket_table_grad: float32 [6144], P('fsdp')
Inputs may be any that keep to these rules, and one draw needn't show every extreme that they name: `segment_ids`: within each packed row page numbers never fall, each page holds 1 to 128 slots, and one page of the row holds exactly 128.
All inputs are finite; a program needn't handle non-finite values.
Results may differ from a plain program's by a relative error of at most 0.017.
Values may be sent and summed in bfloat16 or wider, within the bound.
No kernel may reach another device: no remote copies, remote signals or barrier semaphores. Data moves between devices by JAX's collectives and lax.ppermute only.
A program may use at most 256 MiB of HBM per device.

v0:
```python
import jax
import jax.numpy as jnp
from jax import lax
from jax.sharding import PartitionSpec as P

HEADS = 16
HEAD_DIM = 64
NB = 128


EPSILON = 1e-05
BLOCKED = -1e30


def norm_layer(values, norm_gain, norm_shift):
    center = jnp.mean(values, axis=-1, keepdims=True)
    centered = values - center
    spread = lax.rsqrt(jnp.mean(centered * centered, axis=-1, keepdims=True) + EPSILON)
    return centered * spread * norm_gain + norm_shift


def exact_gelu(values):
    return jax.nn.gelu(values, approximate=False)


def relative(coords, midpoint):
    offsets = coords[None, :] - coords[:, None]
    return jnp.clip(offsets, -midpoint, midpoint - 1) + midpoint


def page_positions(segment_ids):
    slot_count = segment_ids.shape[1]
    slot_index = lax.iota(jnp.int32, slot_count)
    previous = jnp.concatenate([segment_ids[:, :1] - 1, segment_ids[:, :-1]], axis=1)
    starts = jnp.where(segment_ids != previous, slot_index[None, :], 0)
    return slot_index[None, :] - lax.cummax(starts, axis=1)


def bucket_ids(position, box_left, box_top):

    def one_row(row_pos, row_left, row_top):
        return jnp.stack(
            [relative(row_pos, NB // 2), relative(row_left, NB // 2), relative(row_top, NB // 2)]
        )

    return jax.vmap(one_row)(position, box_left, box_top)


def product(left_side, right_side):
    return jnp.dot(left_side, right_side, preferred_element_type=jnp.float32)


def product_back(left_side, right_side):
    return lax.dot_general(
        left_side, right_side, (((1,), (1,)), ((), ())), preferred_element_type=jnp.float32
    )


def weight_grad(left_side, right_side):
    return lax.dot_general(
        left_side, right_side, (((0,), (0,)), ((), ())), preferred_element_type=jnp.float32
    )


def split_blocks(row_ids):
    slot_count = row_ids.shape[-1]
    return row_ids.reshape(3, 8, slot_count // 8, slot_count).transpose(1, 0, 2, 3)


def onehot_of(block_ids):
    return (block_ids[..., None] == lax.iota(jnp.int32, NB)).astype(jnp.bfloat16)


def pair_bias(row_ids, bias_table):
    slot_count = row_ids.shape[-1]

    def pair_one_block(block_ids):
        return jnp.einsum(
            "kqsb,kbh->hqs", onehot_of(block_ids), bias_table, preferred_element_type=jnp.float32
        )

    blocks = lax.map(pair_one_block, split_blocks(row_ids))
    return blocks.transpose(1, 0, 2, 3).reshape(HEADS, slot_count, slot_count)


def table_grad(row_ids, d_logits):
    slot_count = row_ids.shape[-1]
    grad_blocks = d_logits.reshape(HEADS, 8, slot_count // 8, slot_count).transpose(1, 0, 2, 3)

    def table_one_block(running, block_items):
        block_ids, block_grad = block_items
        added = jnp.einsum(
            "kqsb,hqs->kbh", onehot_of(block_ids), block_grad, preferred_element_type=jnp.float32
        )
        return (running + added, None)

    initial = jnp.zeros((3, NB, HEADS), jnp.float32)
    result = lax.scan(table_one_block, initial, (split_blocks(row_ids), grad_blocks))
    return result[0]


def row_logits(row_queries, row_keys, row_ids, row_mask, bias_table):
    score_scale = HEAD_DIM ** (-0.5)
    scores = (
        jnp.einsum("qhe,khe->hqk", row_queries, row_keys, preferred_element_type=jnp.float32)
        * score_scale
    )
    return jnp.where(row_mask[None], scores + pair_bias(row_ids, bias_table), BLOCKED)


def on_device(
    hidden_in,
    cotangent,
    segment_ids,
    box_left,
    box_top,
    query_weight,
    query_bias,
    key_weight,
    value_weight,
    value_bias,
    output_weight,
    output_bias,
    first_gain,
    first_shift,
    inner_weight,
    inner_bias,
    outer_weight,
    outer_bias,
    second_gain,
    second_shift,
    bucket_table,
):
    gathered = (
        lax.all_gather(query_weight, "fsdp", axis=0, tiled=True),
        lax.all_gather(query_bias, "fsdp", axis=0, tiled=True),
        lax.all_gather(key_weight, "fsdp", axis=0, tiled=True),
        lax.all_gather(value_weight, "fsdp", axis=0, tiled=True),
        lax.all_gather(value_bias, "fsdp", axis=0, tiled=True),
        lax.all_gather(output_weight, "fsdp", axis=0, tiled=True),
        lax.all_gather(output_bias, "fsdp", axis=0, tiled=True),
        lax.all_gather(first_gain, "fsdp", axis=0, tiled=True),
        lax.all_gather(first_shift, "fsdp", axis=0, tiled=True),
        lax.all_gather(inner_weight, "fsdp", axis=0, tiled=True),
        lax.all_gather(inner_bias, "fsdp", axis=0, tiled=True),
        lax.all_gather(outer_weight, "fsdp", axis=0, tiled=True),
        lax.all_gather(outer_bias, "fsdp", axis=0, tiled=True),
        lax.all_gather(second_gain, "fsdp", axis=0, tiled=True),
        lax.all_gather(second_shift, "fsdp", axis=0, tiled=True),
        lax.all_gather(bucket_table, "fsdp", axis=0, tiled=True),
    )
    row_count, slot_count = segment_ids.shape
    token_count = hidden_in.shape[0]
    score_scale = HEAD_DIM ** (-0.5)
    by_rows = (row_count, slot_count, HEADS, HEAD_DIM)
    flat_rows = (slot_count, HEADS * HEAD_DIM)
    position = page_positions(segment_ids)
    pair_ids = bucket_ids(position, box_left, box_top)
    page_mask = segment_ids[:, :, None] == segment_ids[:, None, :]
    queries = (product(hidden_in, gathered[0]) + gathered[1]).astype(jnp.bfloat16)
    keys_low = product(hidden_in, gathered[2]).astype(jnp.bfloat16)
    values_low = (product(hidden_in, gathered[3]) + gathered[4]).astype(jnp.bfloat16)
    bias_table = gathered[15].reshape(3, NB, HEADS)

    def attend(row_items):
        row_queries, row_keys, row_values, row_ids, row_mask = row_items
        logits = row_logits(row_queries, row_keys, row_ids, row_mask, bias_table)
        row_peak = jnp.max(logits, axis=-1, keepdims=True)
        weights_exp = jnp.exp(logits - row_peak)
        row_total = jnp.sum(weights_exp, axis=-1, keepdims=True)
        prob_low = (weights_exp / row_total).astype(jnp.bfloat16)
        context_row = jnp.einsum(
            "hqk,khe->qhe", prob_low, row_values, preferred_element_type=jnp.float32
        )
        return (
            context_row.reshape(flat_rows).astype(jnp.bfloat16),
            (row_peak + jnp.log(row_total))[..., 0],
        )

    context, log_total = lax.map(
        attend,
        (
            queries.reshape(by_rows),
            keys_low.reshape(by_rows),
            values_low.reshape(by_rows),
            pair_ids,
            page_mask,
        ),
    )
    context = context.reshape(token_count, HEADS * HEAD_DIM)
    attn_out = product(context, gathered[5]) + gathered[6]
    summed_first = hidden_in.astype(jnp.float32) + attn_out
    first_out = norm_layer(summed_first, gathered[7], gathered[8])
    first_low = first_out.astype(jnp.bfloat16)
    inner = product(first_low, gathered[9]) + gathered[10]
    active = exact_gelu(inner).astype(jnp.bfloat16)
    outer = product(active, gathered[11]) + gathered[12]
    summed_second = first_out + outer
    layer_out = norm_layer(summed_second, gathered[13], gathered[14]).astype(jnp.bfloat16)
    again = (
        lax.all_gather(query_weight, "fsdp", axis=0, tiled=True),
        lax.all_gather(query_bias, "fsdp", axis=0, tiled=True),
        lax.all_gather(key_weight, "fsdp", axis=0, tiled=True),
        lax.all_gather(value_weight, "fsdp", axis=0, tiled=True),
        lax.all_gather(value_bias, "fsdp", axis=0, tiled=True),
        lax.all_gather(output_weight, "fsdp", axis=0, tiled=True),
        lax.all_gather(output_bias, "fsdp", axis=0, tiled=True),
        lax.all_gather(first_gain, "fsdp", axis=0, tiled=True),
        lax.all_gather(first_shift, "fsdp", axis=0, tiled=True),
        lax.all_gather(inner_weight, "fsdp", axis=0, tiled=True),
        lax.all_gather(inner_bias, "fsdp", axis=0, tiled=True),
        lax.all_gather(outer_weight, "fsdp", axis=0, tiled=True),
        lax.all_gather(outer_bias, "fsdp", axis=0, tiled=True),
        lax.all_gather(second_gain, "fsdp", axis=0, tiled=True),
        lax.all_gather(second_shift, "fsdp", axis=0, tiled=True),
        lax.all_gather(bucket_table, "fsdp", axis=0, tiled=True),
    )
    back_table = again[15].reshape(3, NB, HEADS)
    upstream = cotangent.astype(jnp.float32)
    second_pull = jax.vjp(
        norm_layer, summed_second, again[13].astype(jnp.float32), again[14].astype(jnp.float32)
    )[1]
    d_second, second_gain_grad, second_shift_grad = second_pull(upstream)
    d_outer = d_second.astype(jnp.bfloat16)
    outer_bias_grad = jnp.sum(d_outer, axis=0, dtype=jnp.float32)
    outer_weight_grad = weight_grad(active, d_outer)
    gelu_pull = jax.vjp(exact_gelu, inner)[1]
    d_inner = gelu_pull(product_back(d_outer, again[11]))[0].astype(jnp.bfloat16)
    inner_bias_grad = jnp.sum(d_inner, axis=0, dtype=jnp.float32)
    inner_weight_grad = weight_grad(first_low, d_inner)
    d_first = d_second + product_back(d_inner, again[9])
    first_pull = jax.vjp(
        norm_layer, summed_first, again[7].astype(jnp.float32), again[8].astype(jnp.float32)
    )[1]
    d_summed, first_gain_grad, first_shift_grad = first_pull(d_first)
    d_attn = d_summed.astype(jnp.bfloat16)
    output_bias_grad = jnp.sum(d_attn, axis=0, dtype=jnp.float32)
    output_weight_grad = weight_grad(context, d_attn)
    d_context = product_back(d_attn, again[5]).astype(jnp.bfloat16)

    def attend_back(row_items):
        row_queries, row_keys, row_values, row_ids, row_mask, row_log, row_grad = row_items
        logits = row_logits(row_queries, row_keys, row_ids, row_mask, back_table)
        prob_full = jnp.exp(logits - row_log[..., None])
        d_probs = jnp.einsum(
            "qhe,khe->hqk", row_grad, row_values, preferred_element_type=jnp.float32
        )
        inner_sum = jnp.sum(prob_full * d_probs, axis=-1, keepdims=True)
        d_logits = (prob_full * (d_probs - inner_sum)).astype(jnp.bfloat16)
        d_values = jnp.einsum(
            "hqk,qhe->khe",
            prob_full.astype(jnp.bfloat16),
            row_grad,
            preferred_element_type=jnp.float32,
        )
        d_queries = (
            jnp.einsum("hqk,khe->qhe", d_logits, row_keys, preferred_element_type=jnp.float32)
            * score_scale
        )
        d_keys = (
            jnp.einsum("hqk,qhe->khe", d_logits, row_queries, preferred_element_type=jnp.float32)
            * score_scale
        )
        return (
            d_queries.reshape(flat_rows).astype(jnp.bfloat16),
            d_keys.reshape(flat_rows).astype(jnp.bfloat16),
            d_values.reshape(flat_rows).astype(jnp.bfloat16),
            table_grad(row_ids, d_logits),
        )

    row_grads = lax.map(
        attend_back,
        (
            queries.reshape(by_rows),
            keys_low.reshape(by_rows),
            values_low.reshape(by_rows),
            pair_ids,
            page_mask,
            log_total,
            d_context.reshape(by_rows),
        ),
    )
    d_queries = row_grads[0].reshape(token_count, HEADS * HEAD_DIM)
    d_keys = row_grads[1].reshape(token_count, HEADS * HEAD_DIM)
    d_values = row_grads[2].reshape(token_count, HEADS * HEAD_DIM)
    bucket_grad = jnp.sum(row_grads[3], axis=0).reshape(3 * NB * HEADS)
    query_bias_grad = jnp.sum(d_queries, axis=0, dtype=jnp.float32)
    query_weight_grad = weight_grad(hidden_in, d_queries)
    key_weight_grad = weight_grad(hidden_in, d_keys)
    value_bias_grad = jnp.sum(d_values, axis=0, dtype=jnp.float32)
    value_weight_grad = weight_grad(hidden_in, d_values)
    input_grad = (
        d_summed
        + product_back(d_queries, again[0])
        + product_back(d_keys, again[2])
        + product_back(d_values, again[3])
    )
    owned = (
        lax.psum_scatter(query_weight_grad, "fsdp", scatter_dimension=0, tiled=True),
        lax.psum_scatter(query_bias_grad, "fsdp", scatter_dimension=0, tiled=True),
        lax.psum_scatter(key_weight_grad, "fsdp", scatter_dimension=0, tiled=True),
        lax.psum_scatter(value_weight_grad, "fsdp", scatter_dimension=0, tiled=True),
        lax.psum_scatter(value_bias_grad, "fsdp", scatter_dimension=0, tiled=True),
        lax.psum_scatter(output_weight_grad, "fsdp", scatter_dimension=0, tiled=True),
        lax.psum_scatter(output_bias_grad, "fsdp", scatter_dimension=0, tiled=True),
        lax.psum_scatter(first_gain_grad, "fsdp", scatter_dimension=0, tiled=True),
        lax.psum_scatter(first_shift_grad, "fsdp", scatter_dimension=0, tiled=True),
        lax.psum_scatter(inner_weight_grad, "fsdp", scatter_dimension=0, tiled=True),
        lax.psum_scatter(inner_bias_grad, "fsdp", scatter_dimension=0, tiled=True),
        lax.psum_scatter(outer_weight_grad, "fsdp", scatter_dimension=0, tiled=True),
        lax.psum_scatter(outer_bias_grad, "fsdp", scatter_dimension=0, tiled=True),
        lax.psum_scatter(second_gain_grad, "fsdp", scatter_dimension=0, tiled=True),
        lax.psum_scatter(second_shift_grad, "fsdp", scatter_dimension=0, tiled=True),
        lax.psum_scatter(bucket_grad, "fsdp", scatter_dimension=0, tiled=True),
    )
    summed = (
        lax.psum(owned[0].astype(jnp.bfloat16), "dp").astype(jnp.float32),
        lax.psum(owned[1].astype(jnp.bfloat16), "dp").astype(jnp.float32),
        lax.psum(owned[2].astype(jnp.bfloat16), "dp").astype(jnp.float32),
        lax.psum(owned[3].astype(jnp.bfloat16), "dp").astype(jnp.float32),
        lax.psum(owned[4].astype(jnp.bfloat16), "dp").astype(jnp.float32),
        lax.psum(owned[5].astype(jnp.bfloat16), "dp").astype(jnp.float32),
        lax.psum(owned[6].astype(jnp.bfloat16), "dp").astype(jnp.float32),
        lax.psum(owned[7].astype(jnp.bfloat16), "dp").astype(jnp.float32),
        lax.psum(owned[8].astype(jnp.bfloat16), "dp").astype(jnp.float32),
        lax.psum(owned[9].astype(jnp.bfloat16), "dp").astype(jnp.float32),
        lax.psum(owned[10].astype(jnp.bfloat16), "dp").astype(jnp.float32),
        lax.psum(owned[11].astype(jnp.bfloat16), "dp").astype(jnp.float32),
        lax.psum(owned[12].astype(jnp.bfloat16), "dp").astype(jnp.float32),
        lax.psum(owned[13].astype(jnp.bfloat16), "dp").astype(jnp.float32),
        lax.psum(owned[14].astype(jnp.bfloat16), "dp").astype(jnp.float32),
        lax.psum(owned[15].astype(jnp.bfloat16), "dp").astype(jnp.float32),
    )
    return (layer_out, input_grad) + tuple(summed)


def solution(mesh):
    return jax.shard_map(
        on_device,
        mesh=mesh,
        in_specs=(
            P(("fsdp", "dp"), None),
            P(("fsdp", "dp"), None),
            P(("fsdp", "dp"), None),
            P(("fsdp", "dp"), None),
            P(("fsdp", "dp"), None),
            P("fsdp", None),
            P("fsdp"),
            P("fsdp", None),
            P("fsdp", None),
            P("fsdp"),
            P("fsdp", None),
            P("fsdp"),
            P("fsdp"),
            P("fsdp"),
            P("fsdp", None),
            P("fsdp"),
            P("fsdp", None),
            P("fsdp"),
            P("fsdp"),
            P("fsdp"),
            P("fsdp"),
        ),
        out_specs=(
            P(("fsdp", "dp"), None),
            P(("fsdp", "dp"), None),
            P("fsdp", None),
            P("fsdp"),
            P("fsdp", None),
            P("fsdp", None),
            P("fsdp"),
            P("fsdp", None),
            P("fsdp"),
            P("fsdp"),
            P("fsdp"),
            P("fsdp", None),
            P("fsdp"),
            P("fsdp", None),
            P("fsdp"),
            P("fsdp"),
            P("fsdp"),
            P("fsdp"),
        ),
        check_vma=False,
    )
```

profile of v0, /device:TPU:0, one launch (start us, length us, event | category | flops | bytes accessed | tf_op | source)
XLA Modules:
  0.0 1361.1 jit_solution(14414699051095200315)
XLA Ops:
  62.2 239.8 %while.34 = (s32[]{:T(128)}, f32[8,16,68,544]{3,1,2,0:T(8,128)}, s32[8,3,68,544]{3,2,1,0:T(8,128)}, bf16[3,128,16]{1,2,0:T(8,128)(2,1)S(1)}, s32[]{:T(128)}) while((s32[]{:T(128)}, f32[8,16,68,544]{3,1,2,0:T(8,128)}, s32[8,3,68,544]{3,2,1,0:T(8,128)}, bf16[3,128,16]{1,2,0:T(8,128)(2,1)S(1)}, s32[]{:T(128)}) %tuple.72), condition=%wide.region_3.4_spmd, body=%wide.region_2.3_spmd.sunk | while | flops 468762624 | bytes 5017165 | solution.py:82
  63.6 28.7 %bitcast_dynamic-update-slice_fusion.2 = f32[8,16,68,544]{3,1,2,0:T(8,128)} fusion(f32[8,16,68,544]{3,1,2,0:T(8,128)} %get-tuple-element.356, s32[]{:T(128)S(6)} %copy.94, s32[3,68,544]{2,0,1:T(4,128)S(1)} %bitcast.162, bf16[3,128,16]{1,2,0:T(8,128)(2,1)S(1)} %get-tuple-element.363), kind=kOutput, calls=%fused_computation.3.clone.2 | convolution fusion | flops 468762624 | bytes 3241476 | tf_op jit(solution)/shard_map/while/body/eval_jaxpr/while/body/eval_jaxpr/kqsb,kbh->hqs/dot_general | solution.py:78
  93.5 28.7 %bitcast_dynamic-update-slice_fusion.2 = f32[8,16,68,544]{3,1,2,0:T(8,128)} fusion(f32[8,16,68,544]{3,1,2,0:T(8,128)} %get-tuple-element.356, s32[]{:T(128)S(6)} %copy.94, s32[3,68,544]{2,0,1:T(4,128)S(1)} %bitcast.162, bf16[3,128,16]{1,2,0:T(8,128)(2,1)S(1)} %get-tuple-element.363), kind=kOutput, calls=%fused_computation.3.clone.2 | convolution fusion | flops 468762624 | bytes 3241476 | tf_op jit(solution)/shard_map/while/body/eval_jaxpr/while/body/eval_jaxpr/kqsb,kbh->hqs/dot_general | solution.py:78
  123.5 28.7 %bitcast_dynamic-update-slice_fusion.2 = f32[8,16,68,544]{3,1,2,0:T(8,128)} fusion(f32[8,16,68,544]{3,1,2,0:T(8,128)} %get-tuple-element.356, s32[]{:T(128)S(6)} %copy.94, s32[3,68,544]{2,0,1:T(4,128)S(1)} %bitcast.162, bf16[3,128,16]{1,2,0:T(8,128)(2,1)S(1)} %get-tuple-element.363), kind=kOutput, calls=%fused_computation.3.clone.2 | convolution fusion | flops 468762624 | bytes 3241476 | tf_op jit(solution)/shard_map/while/body/eval_jaxpr/while/body/eval_jaxpr/kqsb,kbh->hqs/dot_general | solution.py:78
  153.4 28.7 %bitcast_dynamic-update-slice_fusion.2 = f32[8,16,68,544]{3,1,2,0:T(8,128)} fusion(f32[8,16,68,544]{3,1,2,0:T(8,128)} %get-tuple-element.356, s32[]{:T(128)S(6)} %copy.94, s32[3,68,544]{2,0,1:T(4,128)S(1)} %bitcast.162, bf16[3,128,16]{1,2,0:T(8,128)(2,1)S(1)} %get-tuple-element.363), kind=kOutput, calls=%fused_computation.3.clone.2 | convolution fusion | flops 468762624 | bytes 3241476 | tf_op jit(solution)/shard_map/while/body/eval_jaxpr/while/body/eval_jaxpr/kqsb,kbh->hqs/dot_general | solution.py:78
  183.4 28.7 %bitcast_dynamic-update-slice_fusion.2 = f32[8,16,68,544]{3,1,2,0:T(8,128)} fusion(f32[8,16,68,544]{3,1,2,0:T(8,128)} %get-tuple-element.356, s32[]{:T(128)S(6)} %copy.94, s32[3,68,544]{2,0,1:T(4,128)S(1)} %bitcast.162, bf16[3,128,16]{1,2,0:T(8,128)(2,1)S(1)} %get-tuple-element.363), kind=kOutput, calls=%fused_computation.3.clone.2 | convolution fusion | flops 468762624 | bytes 3241476 | tf_op jit(solution)/shard_map/while/body/eval_jaxpr/while/body/eval_jaxpr/kqsb,kbh->hqs/dot_general | solution.py:78
  213.3 28.7 %bitcast_dynamic-update-slice_fusion.2 = f32[8,16,68,544]{3,1,2,0:T(8,128)} fusion(f32[8,16,68,544]{3,1,2,0:T(8,128)} %get-tuple-element.356, s32[]{:T(128)S(6)} %copy.94, s32[3,68,544]{2,0,1:T(4,128)S(1)} %bitcast.162, bf16[3,128,16]{1,2,0:T(8,128)(2,1)S(1)} %get-tuple-element.363), kind=kOutput, calls=%fused_computation.3.clone.2 | convolution fusion | flops 468762624 | bytes 3241476 | tf_op jit(solution)/shard_map/while/body/eval_jaxpr/while/body/eval_jaxpr/kqsb,kbh->hqs/dot_general | solution.py:78
  243.4 28.7 %bitcast_dynamic-update-slice_fusion.2 = f32[8,16,68,544]{3,1,2,0:T(8,128)} fusion(f32[8,16,68,544]{3,1,2,0:T(8,128)} %get-tuple-element.356, s32[]{:T(128)S(6)} %copy.94, s32[3,68,544]{2,0,1:T(4,128)S(1)} %bitcast.162, bf16[3,128,16]{1,2,0:T(8,128)(2,1)S(1)} %get-tuple-element.363), kind=kOutput, calls=%fused_computation.3.clone.2 | convolution fusion | flops 468762624 | bytes 3241476 | tf_op jit(solution)/shard_map/while/body/eval_jaxpr/while/body/eval_jaxpr/kqsb,kbh->hqs/dot_general | solution.py:78
  273.3 28.7 %bitcast_dynamic-update-slice_fusion.2 = f32[8,16,68,544]{3,1,2,0:T(8,128)} fusion(f32[8,16,68,544]{3,1,2,0:T(8,128)} %get-tuple-element.356, s32[]{:T(128)S(6)} %copy.94, s32[3,68,544]{2,0,1:T(4,128)S(1)} %bitcast.162, bf16[3,128,16]{1,2,0:T(8,128)(2,1)S(1)} %get-tuple-element.363), kind=kOutput, calls=%fused_computation.3.clone.2 | convolution fusion | flops 468762624 | bytes 3241476 | tf_op jit(solution)/shard_map/while/body/eval_jaxpr/while/body/eval_jaxpr/kqsb,kbh->hqs/dot_general | solution.py:78
  407.7 29.3 %multiply_convert_fusion.1 = (bf16[544,4096]{1,0:T(8,128)(2,1)}, f32[544,4096]{1,0:T(8,128)}, f32[544,4096]{1,0:T(8,128)}) fusion(f32[4096]{0:T(1024)} %bitcast.180, bf16[1024,4096]{1,0:T(8,128)(2,1)} %all-gather.25.cloned.1.call-done, f32[544,1024]{1,0:T(8,128)S(1)} %get-tuple-element.285, f32[1024]{0:T(1024)} %bitcast.189, f32[1024]{0:T(1024)S(1)} %bitcast.184, ...), kind=kOutput, calls=%fused_computation.32 | convolution fusion | flops 4713250816 | bytes 32928000 | tf_op jit(solution)/shard_map/dot_general | solution.py:50
  610.1 25.4 %reduce-scatter.9.cloned.1.call-done = f32[128,1024]{0,1:T(8,128)} async-done(((f32[1024,1024]{0,1:T(8,128)}), f32[128,1024]{0,1:T(8,128)}) %reduce-scatter.9.cloned.1.call-update) | async-done | bytes 524304 | tf_op jit(solution)/shard_map/reduce_scatter | solution.py:301
  637.3 52.9 %reduce-scatter.11.cloned.1.call-done = f32[128,1024]{0,1:T(8,128)} async-done(((f32[1024,1024]{0,1:T(8,128)}), f32[128,1024]{0,1:T(8,128)}) %reduce-scatter.11.cloned.1.call-update) | async-done | bytes 524304 | tf_op jit(solution)/shard_map/reduce_scatter | solution.py:302
  691.9 53.2 %reduce-scatter.13.cloned.1.call-done = f32[128,1024]{1,0:T(8,128)} async-done(((f32[1024,1024]{1,0:T(8,128)}), f32[128,1024]{1,0:T(8,128)}) %reduce-scatter.13.cloned.1.call-update) | async-done | bytes 524304 | tf_op jit(solution)/shard_map/reduce_scatter | solution.py:304
  746.9 117.8 %reduce-scatter.15.cloned.1.call-done = f32[128,4096]{1,0:T(8,128)} async-done(((f32[1024,4096]{1,0:T(8,128)}), f32[128,4096]{1,0:T(8,128)}) %reduce-scatter.15.cloned.1.call-update) | async-done | bytes 2097168 | tf_op jit(solution)/shard_map/reduce_scatter | solution.py:308
  867.4 116.7 %reduce-scatter.17.cloned.1.call-done = f32[512,1024]{1,0:T(8,128)} async-done(((f32[4096,1024]{1,0:T(8,128)}), f32[512,1024]{1,0:T(8,128)}) %reduce-scatter.17.cloned.1.call-update) | async-done | bytes 2097168 | tf_op jit(solution)/shard_map/reduce_scatter | solution.py:310
  986.9 306.2 %while.35 = (s32[]{:T(128)}, f32[3,128,16]{1,2,0:T(8,128)S(1)}, s32[8,3,68,544]{3,2,1,0:T(8,128)}, bf16[8,16,68,544]{3,1,2,0:T(8,128)(2,1)}, s32[]{:T(128)}, /*index=5*/s32[]{:T(128)}) while((s32[]{:T(128)}, f32[3,128,16]{1,2,0:T(8,128)S(1)}, s32[8,3,68,544]{3,2,1,0:T(8,128)}, bf16[8,16,68,544]{3,1,2,0:T(8,128)(2,1)}, ...), condition=%wide.region_55.56_spmd.clone, body=%wide.region_54.55_spmd.clone.sunk | while | flops 468774912 | bytes 4932191 | solution.py:98
  989.6 35.7 %fusion.112 = f32[3,128,16]{1,2,0:T(8,128)S(1)} fusion(s32[3,68,544]{2,1,0:T(8,128)S(1)} %dynamic-slice_bitcast_fusion.2, f32[3,128,16]{1,2,0:T(8,128)S(1)} %get-tuple-element.372, pred[]{:T(512)S(6)} %compare.4, bf16[16,68,544,1]{2,0,1,3:T(8,128)(2,1)S(1)} %fusion.111), kind=kOutput, calls=%fused_computation.13.clone.3 | convolution fusion | flops 468774912 | bytes 1676801 | tf_op jit(solution)/shard_map/while/body/eval_jaxpr/while/body/eval_jaxpr/kqsb,hqs->kbh/dot_general | solution.py:92
  1027.8 35.7 %fusion.112 = f32[3,128,16]{1,2,0:T(8,128)S(1)} fusion(s32[3,68,544]{2,1,0:T(8,128)S(1)} %dynamic-slice_bitcast_fusion.2, f32[3,128,16]{1,2,0:T(8,128)S(1)} %get-tuple-element.372, pred[]{:T(512)S(6)} %compare.4, bf16[16,68,544,1]{2,0,1,3:T(8,128)(2,1)S(1)} %fusion.111), kind=kOutput, calls=%fused_computation.13.clone.3 | convolution fusion | flops 468774912 | bytes 1676801 | tf_op jit(solution)/shard_map/while/body/eval_jaxpr/while/body/eval_jaxpr/kqsb,hqs->kbh/dot_general | solution.py:92
  1066.1 35.7 %fusion.112 = f32[3,128,16]{1,2,0:T(8,128)S(1)} fusion(s32[3,68,544]{2,1,0:T(8,128)S(1)} %dynamic-slice_bitcast_fusion.2, f32[3,128,16]{1,2,0:T(8,128)S(1)} %get-tuple-element.372, pred[]{:T(512)S(6)} %compare.4, bf16[16,68,544,1]{2,0,1,3:T(8,128)(2,1)S(1)} %fusion.111), kind=kOutput, calls=%fused_computation.13.clone.3 | convolution fusion | flops 468774912 | bytes 1676801 | tf_op jit(solution)/shard_map/while/body/eval_jaxpr/while/body/eval_jaxpr/kqsb,hqs->kbh/dot_general | solution.py:92
  1104.4 35.7 %fusion.112 = f32[3,128,16]{1,2,0:T(8,128)S(1)} fusion(s32[3,68,544]{2,1,0:T(8,128)S(1)} %dynamic-slice_bitcast_fusion.2, f32[3,128,16]{1,2,0:T(8,128)S(1)} %get-tuple-element.372, pred[]{:T(512)S(6)} %compare.4, bf16[16,68,544,1]{2,0,1,3:T(8,128)(2,1)S(1)} %fusion.111), kind=kOutput, calls=%fused_computation.13.clone.3 | convolution fusion | flops 468774912 | bytes 1676801 | tf_op jit(solution)/shard_map/while/body/eval_jaxpr/while/body/eval_jaxpr/kqsb,hqs->kbh/dot_general | solution.py:92
  1142.6 35.7 %fusion.112 = f32[3,128,16]{1,2,0:T(8,128)S(1)} fusion(s32[3,68,544]{2,1,0:T(8,128)S(1)} %dynamic-slice_bitcast_fusion.2, f32[3,128,16]{1,2,0:T(8,128)S(1)} %get-tuple-element.372, pred[]{:T(512)S(6)} %compare.4, bf16[16,68,544,1]{2,0,1,3:T(8,128)(2,1)S(1)} %fusion.111), kind=kOutput, calls=%fused_computation.13.clone.3 | convolution fusion | flops 468774912 | bytes 1676801 | tf_op jit(solution)/shard_map/while/body/eval_jaxpr/while/body/eval_jaxpr/kqsb,hqs->kbh/dot_general | solution.py:92
  1180.9 35.7 %fusion.112 = f32[3,128,16]{1,2,0:T(8,128)S(1)} fusion(s32[3,68,544]{2,1,0:T(8,128)S(1)} %dynamic-slice_bitcast_fusion.2, f32[3,128,16]{1,2,0:T(8,128)S(1)} %get-tuple-element.372, pred[]{:T(512)S(6)} %compare.4, bf16[16,68,544,1]{2,0,1,3:T(8,128)(2,1)S(1)} %fusion.111), kind=kOutput, calls=%fused_computation.13.clone.3 | convolution fusion | flops 468774912 | bytes 1676801 | tf_op jit(solution)/shard_map/while/body/eval_jaxpr/while/body/eval_jaxpr/kqsb,hqs->kbh/dot_general | solution.py:92
  1219.1 35.7 %fusion.112 = f32[3,128,16]{1,2,0:T(8,128)S(1)} fusion(s32[3,68,544]{2,1,0:T(8,128)S(1)} %dynamic-slice_bitcast_fusion.2, f32[3,128,16]{1,2,0:T(8,128)S(1)} %get-tuple-element.372, pred[]{:T(512)S(6)} %compare.4, bf16[16,68,544,1]{2,0,1,3:T(8,128)(2,1)S(1)} %fusion.111), kind=kOutput, calls=%fused_computation.13.clone.3 | convolution fusion | flops 468774912 | bytes 1676801 | tf_op jit(solution)/shard_map/while/body/eval_jaxpr/while/body/eval_jaxpr/kqsb,hqs->kbh/dot_general | solution.py:92
  1257.4 35.7 %fusion.112 = f32[3,128,16]{1,2,0:T(8,128)S(1)} fusion(s32[3,68,544]{2,1,0:T(8,128)S(1)} %dynamic-slice_bitcast_fusion.2, f32[3,128,16]{1,2,0:T(8,128)S(1)} %get-tuple-element.372, pred[]{:T(512)S(6)} %compare.4, bf16[16,68,544,1]{2,0,1,3:T(8,128)(2,1)S(1)} %fusion.111), kind=kOutput, calls=%fused_computation.13.clone.3 | convolution fusion | flops 468774912 | bytes 1676801 | tf_op jit(solution)/shard_map/while/body/eval_jaxpr/while/body/eval_jaxpr/kqsb,hqs->kbh/dot_general | solution.py:92
  (318 shorter events, 433.3 us)
Async XLA Ops:
  7.3 338.8 %all-gather.19.cloned.1.call-start = ((), (), s32[]{:S(2)}) async-start(), calls=%async_computation.7 | async-start | bytes 2359296 | tf_op jit(solution)/shard_map/all_gather | solution.py:135
  8.0 343.7 %all-gather.21.cloned.1.call-start = ((), (), s32[]{:S(2)}) async-start(), calls=%async_computation.8 | async-start | bytes 2359296 | tf_op jit(solution)/shard_map/all_gather | solution.py:137
  8.8 369.2 %all-gather.17.cloned.1.call-start = ((), (), s32[]{:S(2)}) async-start(), calls=%async_computation.6 | async-start | bytes 2359296 | tf_op jit(solution)/shard_map/all_gather | solution.py:138
  9.5 392.4 %all-gather.23.cloned.1.call-start = ((), (), s32[]{:S(2)}) async-start(), calls=%async_computation.9 | async-start | bytes 2359296 | tf_op jit(solution)/shard_map/all_gather | solution.py:140
  10.1 397.6 %all-gather.25.cloned.1.call-start = ((), (), s32[]{:S(2)}) async-start(), calls=%async_computation.10 | async-start | bytes 9437184 | tf_op jit(solution)/shard_map/all_gather | solution.py:144
  10.7 426.3 %all-gather.27.cloned.1.call-start = ((), (), s32[]{:S(2)}) async-start(), calls=%async_computation.11 | async-start | bytes 9437184 | tf_op jit(solution)/shard_map/all_gather | solution.py:146
  11.2 597.1 %reduce-scatter.7.cloned.1.call-start = ((), (), s32[]{:S(2)}) async-start(), calls=%async_computation.12 | async-start | bytes 4718592 | tf_op jit(solution)/shard_map/reduce_scatter | solution.py:299
  62.1 274.3 %copy-start.58 = (bf16[128]{0:T(256)(128)(2,1)S(1)}, bf16[128]{0:T(256)(128)(2,1)}, u32[]{:S(2)}) copy-start(bf16[128]{0:T(256)(128)(2,1)} %param.44) | copy-start | bytes 772
  62.2 283.9 %copy-start.16 = (bf16[544,1024]{1,0:T(8,128)(2,1)S(1)}, bf16[544,1024]{1,0:T(8,128)(2,1)}, u32[]{:S(2)}) copy-start(bf16[544,1024]{1,0:T(8,128)(2,1)} %param.25) | copy-start | bytes 3342340
  528.7 106.7 %reduce-scatter.9.cloned.1.call-start = ((), (), s32[]{:S(2)}) async-start(), calls=%async_computation.13 | async-start | bytes 4718592 | tf_op jit(solution)/shard_map/reduce_scatter | solution.py:301
  541.3 148.9 %reduce-scatter.11.cloned.1.call-start = ((), (), s32[]{:S(2)}) async-start(), calls=%async_computation.14 | async-start | bytes 4718592 | tf_op jit(solution)/shard_map/reduce_scatter | solution.py:302
  556.8 188.4 %reduce-scatter.13.cloned.1.call-start = ((), (), s32[]{:S(2)}) async-start(), calls=%async_computation.15 | async-start | bytes 4718592 | tf_op jit(solution)/shard_map/reduce_scatter | solution.py:304
  563.2 301.5 %reduce-scatter.15.cloned.1.call-start = ((), (), s32[]{:S(2)}) async-start(), calls=%async_computation.16 | async-start | bytes 18874368 | tf_op jit(solution)/shard_map/reduce_scatter | solution.py:308
  578.1 406.0 %reduce-scatter.17.cloned.1.call-start = ((), (), s32[]{:S(2)}) async-start(), calls=%async_computation.17 | async-start | bytes 18874368 | tf_op jit(solution)/shard_map/reduce_scatter | solution.py:310
  592.2 752.4 %all-reduce.16.cloned.1.call-start = ((), (), s32[]{:S(2)}) async-start(), calls=%async_computation.18 | async-start | bytes 6291456 | tf_op jit(solution)/shard_map/psum | solution.py:317
  986.8 306.3 %copy-start.33 = (f32[16,64]{1,0:T(8,128)S(1)}, f32[16,64]{1,0:T(8,128)}, u32[]{:S(2)}) copy-start(f32[16,64]{1,0:T(8,128)} %get-tuple-element.294) | copy-start | bytes 12292
  986.8 306.6 %copy-start.34 = (f32[1024]{0:T(1024)S(1)}, f32[1024]{0:T(1024)}, u32[]{:S(2)}) copy-start(f32[1024]{0:T(1024)} %get-tuple-element.221) | copy-start | bytes 12292
  986.8 306.6 %copy-start.35 = (f32[1024]{0:T(1024)S(1)}, f32[1024]{0:T(1024)}, u32[]{:S(2)}) copy-start(f32[1024]{0:T(1024)} %get-tuple-element.224) | copy-start | bytes 12292
  986.8 306.6 %copy-start.36 = (f32[1024]{0:T(1024)S(1)}, f32[1024]{0:T(1024)}, u32[]{:S(2)}) copy-start(f32[1024]{0:T(1024)} %get-tuple-element.267) | copy-start | bytes 12292
  986.9 306.6 %copy-start.37 = (f32[1024]{0:T(1024)S(1)}, f32[1024]{0:T(1024)}, u32[]{:S(2)}) copy-start(f32[1024]{0:T(1024)} %get-tuple-element.271) | copy-start | bytes 12292
  986.9 306.6 %copy-start.40 = (f32[4096]{0:T(1024)S(1)}, f32[4096]{0:T(1024)}, u32[]{:S(2)}) copy-start(f32[4096]{0:T(1024)} %get-tuple-element.269) | copy-start | bytes 49156
  986.9 306.6 %copy-start.45 = (f32[1024]{0:T(1024)S(1)}, f32[1024]{0:T(1024)}, u32[]{:S(2)}) copy-start(f32[1024]{0:T(1024)} %get-tuple-element.219) | copy-start | bytes 12292
  986.9 306.6 %copy-start.46 = (f32[1024]{0:T(1024)S(1)}, f32[1024]{0:T(1024)}, u32[]{:S(2)}) copy-start(f32[1024]{0:T(1024)} %get-tuple-element.223) | copy-start | bytes 12292
  986.9 348.7 %copy-start.13 = (bf16[16,64,544]{2,1,0:T(8,128)(2,1)S(1)}, bf16[16,64,544]{2,1,0:T(8,128)(2,1)}, u32[]{:S(2)}) copy-start(bf16[16,64,544]{2,1,0:T(8,128)(2,1)} %copy-done.12) | copy-start | bytes 3342340
  (50 other events, 1522.6 us)
Sparse Core Ops, SparseCore 0:
  10.0 30.5 all-gather.18
  42.5 28.0 all-gather.20
  72.5 28.2 all-gather.16
  102.5 28.2 all-gather.22
  132.5 54.3 all-gather.24
  188.6 54.9 all-gather.26
  528.8 51.4 reduce-scatter.6
  584.1 51.3 reduce-scatter.8
  638.8 51.2 reduce-scatter.10
  693.7 51.3 reduce-scatter.12
  748.7 115.9 reduce-scatter.14
  868.1 115.9 reduce-scatter.16
  988.1 122.9 all-reduce.15
where the time goes:
time: 1370 us; the launch traced here: 1360 us
  matrix products  720 us (53%)
  waiting for transfers between devices  370 us (27%)
  blocking collectives  122 us (9%)
  local copies, waits for them, and re-layouts  70.8 us (5%)
  other arithmetic  60.9 us (4%)
  between operations  17.5 us (1%)
    dot_general x8, matrix products, table_one_block(): jnp.einsum('kqsb,hqs->kbh', onehot_of(block_ids), block_grad, preferred_e...  285 us
    dot_general x8, matrix products, pair_one_block(): jnp.einsum('kqsb,kbh->hqs', onehot_of(block_ids), bias_table, preferred_e...  229 us
    reduce_scatter x1, waiting for transfers between devices, on_device(): lax.psum_scatter(inner_weight_grad, 'fsdp', scatter_dimension=0, tiled=True)  118 us
    reduce_scatter x1, waiting for transfers between devices, on_device(): lax.psum_scatter(outer_weight_grad, 'fsdp', scatter_dimension=0, tiled=True)  117 us
    dot_general x6, matrix products, product(): return jnp.dot(left_side, right_side, preferred_element_type=jnp.float32)  53.5 us
    reduce_scatter x1, waiting for transfers between devices, on_device(): lax.psum_scatter(output_weight_grad, 'fsdp', scatter_dimension=0, tiled=T...  53.2 us
    reduce_scatter x1, waiting for transfers between devices, on_device(): lax.psum_scatter(value_weight_grad, 'fsdp', scatter_dimension=0, tiled=True)  52.9 us
    dot_general x6, matrix products, weight_grad(): lax.dot_general(left_side, right_side, (((0,), (0,)), ((), ())), preferre...  44.3 us
  transfers between devices with their start and end apart: 13, of which 5 were waited for; matrix products, arithmetic and copies ran while one was open for 54% of the time, Pallas kernels for 0%

commit v1 on v0

v1 whole, which is shorter than its diff:
```python
from functools import partial

import jax
import jax.numpy as jnp
import numpy as np
from jax import lax
from jax.experimental import pallas as pl
from jax.experimental.pallas import tpu as pltpu
from jax.sharding import PartitionSpec as P

HEADS = 16
HEAD_DIM = 64
PAIRS = HEADS // 2
NB = 128
PAGE = 128
PAGES = 8
EPSILON = 1e-05
BLOCKED = -1e30
BF = jnp.bfloat16
F32 = jnp.float32
VMEM_LIMIT = 48 * 1024 * 1024
NT = (((1,), (1,)), ((), ()))
TN = (((0,), (0,)), ((), ()))


def dot(left_side, right_side, dims=(((1,), (0,)), ((), ()))):
    return lax.dot_general(left_side, right_side, dims, preferred_element_type=F32)


def flips(bit_of):
    return [(i, i ^ bit_of(i & 1)) for i in range(8)]


NEAR = flips(lambda c: 2 if c else 4)
FAR = flips(lambda c: 4 if c else 2)
TWIN = flips(lambda c: 1)


def block_order(me):
    rel0 = np.array([0, 4, 2, 6, 1, 3, 5, 7], np.int32)
    rel1 = np.array([0, 2, 4, 6, 1, 5, 3, 7], np.int32)
    rel = jnp.where((me & 1) == 0, rel0, rel1)
    return jnp.bitwise_xor(me, rel).astype(jnp.int32)


def hop(value, pairs):
    return lax.ppermute(value, "fsdp", pairs)


def gather_blocks(own):
    near = hop(own, NEAR)
    far = hop(own, FAR)
    both = hop(near, FAR)
    mine = [own, near, far, both]
    return mine + [hop(item, TWIN) for item in mine]


def scatter_blocks(keep, send):
    other = hop(send, TWIN)
    away = keep[2:] + other[2:]
    stay = keep[:2] + other[:2]
    other = hop(away, FAR)
    away = stay[1] + other[1]
    stay = stay[0] + other[0]
    return stay + hop(away, NEAR)


def sum_line(value):
    rows = value.shape[0] // 4
    quarters = value.reshape((4, rows) + value.shape[1:])
    at = lax.axis_index("dp")

    def take(index):
        return lax.dynamic_index_in_dim(quarters, jnp.clip(index, 0, 3), 0, keepdims=False)

    up, down = take(at + 3), take(at - 3)
    for t in range(1, 4):
        up = lax.ppermute(up, "dp", [(i, i + 1) for i in range(t)])
        down = lax.ppermute(down, "dp", [(3 - i, 2 - i) for i in range(t)])
        if t < 3:
            up = up + take(at + 3 - t)
            down = down + take(at - 3 + t)
    mine = take(at) + up + down
    ups, downs = [mine], [mine]
    for t in range(1, 4):
        ups.append(lax.ppermute(ups[-1], "dp", [(i, i + 1) for i in range(t - 1, 3)]))
        downs.append(lax.ppermute(downs[-1], "dp", [(i, i - 1) for i in range(1, 5 - t)]))
    parts = []
    for q in range(4):
        part = mine
        for t in range(1, 4):
            part = jnp.where(at - q == t, ups[t], part)
            part = jnp.where(q - at == t, downs[t], part)
        parts.append(part)
    return jnp.concatenate(parts, axis=0)


def sum_line_small(value):
    value = value + lax.ppermute(value, "dp", [(i, i ^ 1) for i in range(4)])
    return value + lax.ppermute(value, "dp", [(i, i ^ 2) for i in range(4)])


def place_kernel(parts, order_ref, *refs):
    blocks, outs, sem = refs[:8], refs[8:-1], refs[-1]
    rows = blocks[0].shape[0] // parts
    columns = blocks[0].shape[1]
    copies = []
    for k in range(8):
        start = pl.multiple_of(order_ref[k] * rows, rows)
        for j in range(parts):
            copies.append(
                pltpu.make_async_copy(
                    blocks[k].at[pl.ds(j * rows, rows), :],
                    outs[0].at[pl.ds(start, rows), pl.ds(j * columns, columns)],
                    sem.at[k, j],
                )
            )
    for copy in copies:
        copy.start()
    for copy in copies:
        copy.wait()


def place(order, blocks, parts=1):
    rows, columns = blocks[0].shape
    return pl.pallas_call(
        partial(place_kernel, parts),
        out_shape=jax.ShapeDtypeStruct((8 * rows // parts, parts * columns), blocks[0].dtype),
        in_specs=[pl.BlockSpec(memory_space=pltpu.SMEM)]
        + [pl.BlockSpec(memory_space=pl.ANY)] * 8,
        out_specs=pl.BlockSpec(memory_space=pl.ANY),
        scratch_shapes=[pltpu.SemaphoreType.DMA((8, parts))],
        cost_estimate=pl.CostEstimate(
            flops=0, bytes_accessed=32 * rows * columns, transcendentals=0
        ),
    )(order, *blocks)


def pick_kernel(order_ref, grad_ref, keep_ref, send_ref, sem):
    rows = keep_ref.shape[1]
    copies = []
    for k in range(8):
        start = pl.multiple_of(order_ref[k] * rows, rows)
        target = keep_ref if k < 4 else send_ref
        copies.append(
            pltpu.make_async_copy(
                grad_ref.at[pl.ds(start, rows), :], target.at[k % 4], sem.at[k]
            )
        )
    for copy in copies:
        copy.start()
    for copy in copies:
        copy.wait()


def pick(order, grad):
    rows, columns = grad.shape[0] // 8, grad.shape[1]
    shape = jax.ShapeDtypeStruct((4, rows, columns), grad.dtype)
    return pl.pallas_call(
        pick_kernel,
        out_shape=(shape, shape),
        in_specs=[
            pl.BlockSpec(memory_space=pltpu.SMEM),
            pl.BlockSpec(memory_space=pl.ANY),
        ],
        out_specs=(pl.BlockSpec(memory_space=pl.ANY),) * 2,
        scratch_shapes=[pltpu.SemaphoreType.DMA((8,))],
        cost_estimate=pl.CostEstimate(
            flops=0, bytes_accessed=32 * rows * columns, transcendentals=0
        ),
    )(order, grad)


def tables_kernel(position_ref, box_ref, lookup_ref, slide_ref):
    row = lax.broadcasted_iota(jnp.int32, (NB, NB), 0)
    lane = lax.broadcasted_iota(jnp.int32, (NB, NB), 1)
    same = (row < 64) == (lane < 64)
    for head in range(HEADS):
        base = jnp.broadcast_to(position_ref[head : head + 1, :], (PAGE, 2 * PAGE))
        slid = pltpu.roll(base, 0, 1, stride=1, stride_axis=0)
        half = (head % 2) * PAGE
        slide_ref[head // 2, :, half : half + PAGE] = slid[:, :PAGE]
        left = jnp.broadcast_to(box_ref[0, head : head + 1, :], (64, NB))
        top = jnp.broadcast_to(box_ref[1, head : head + 1, :], (64, NB))
        slid = pltpu.roll(
            jnp.concatenate([left, top], axis=0), 0, 1, stride=1, stride_axis=0
        )
        lookup_ref[:, head * NB : (head + 1) * NB] = jnp.where(same, slid, 0.0).astype(BF)


def make_tables(table):
    spot = np.zeros((2 * PAGE, NB), np.float32)
    for m in range(2 * PAGE):
        offset = -m if m <= PAGE else 2 * PAGE - m
        spot[m, min(max(offset, -64), 63) + 64] = 1.0
    position = lax.dot_general(
        table[0], jnp.asarray(spot, BF), (((0,), (1,)), ((), ())), preferred_element_type=F32
    )
    box = jnp.roll(table[1:].astype(F32).transpose(0, 2, 1), 64, axis=2)
    return pl.pallas_call(
        tables_kernel,
        out_shape=(
            jax.ShapeDtypeStruct((NB, HEADS * NB), BF),
            jax.ShapeDtypeStruct((PAIRS, PAGE, 2 * PAGE), F32),
        ),
    )(position, box)


def split_heads(tile):
    lane = lax.broadcasted_iota(jnp.int32, tile.shape, 1)
    zero = jnp.zeros_like(tile)
    return jnp.concatenate(
        [jnp.where(lane < HEAD_DIM, tile, zero), jnp.where(lane >= HEAD_DIM, tile, zero)],
        axis=0,
    )


def join_heads(tall):
    lane = lax.broadcasted_iota(jnp.int32, (PAGE, NB), 1)
    return jnp.where(lane < HEAD_DIM, tall[:PAGE, :NB], tall[PAGE:, :NB])


def attend_kernel(
    length_ref, q_ref, k_ref, v_ref, box_ref, lookup_ref, slide_ref, context_ref, prob_ref
):
    length = length_ref[pl.program_id(0)]
    inside = lax.broadcasted_iota(jnp.int32, (PAGE, 2 * PAGE), 0) < length
    boxes = box_ref[...]
    for pair in range(PAIRS):
        at = slice(pair * NB, (pair + 1) * NB)
        looked = dot(boxes, lookup_ref[:, 2 * pair * NB : 2 * (pair + 1) * NB]).astype(BF)
        looked = jnp.concatenate([looked[:, :NB], looked[:, NB:]], axis=0)
        asked = jnp.concatenate([split_heads(q_ref[:, at]), looked], axis=1)
        offered = jnp.concatenate([k_ref[:, at], boxes], axis=1)
        logits = dot(offered, asked, NT) + slide_ref[pair]
        logits = jnp.where(inside, logits, BLOCKED)
        peak = jnp.max(logits, axis=0, keepdims=True)
        grown = jnp.exp(logits - peak)
        total = jnp.sum(grown, axis=0, keepdims=True)
        prob = (grown * (1.0 / total)).astype(BF)
        prob_ref[0, pair] = prob
        context_ref[:, at] = join_heads(dot(prob, v_ref[:, at], TN)).astype(BF)


def attend(lengths, queries, keys, values, boxes, lookup, slide):
    wide = pl.BlockSpec((PAGE, HEADS * HEAD_DIM), lambda i, n: (i, 0))
    return pl.pallas_call(
        attend_kernel,
        grid_spec=pltpu.PrefetchScalarGridSpec(
            num_scalar_prefetch=1,
            grid=(PAGES,),
            in_specs=[
                wide,
                wide,
                wide,
                pl.BlockSpec((PAGE, NB), lambda i, n: (i, 0)),
                pl.BlockSpec((NB, HEADS * NB), lambda i, n: (0, 0)),
                pl.BlockSpec((PAIRS, PAGE, 2 * PAGE), lambda i, n: (0, 0, 0)),
            ],
            out_specs=(
                wide,
                pl.BlockSpec((1, PAIRS, PAGE, 2 * PAGE), lambda i, n: (i, 0, 0, 0)),
            ),
        ),
        out_shape=(
            jax.ShapeDtypeStruct((PAGES * PAGE, HEADS * HEAD_DIM), BF),
            jax.ShapeDtypeStruct((PAGES, PAIRS, PAGE, 2 * PAGE), BF),
        ),
        compiler_params=pltpu.CompilerParams(vmem_limit_bytes=VMEM_LIMIT),
        cost_estimate=pl.CostEstimate(
            flops=6 * 10**9, bytes_accessed=14 * 2**20, transcendentals=2 * 2**20
        ),
    )(lengths, queries, keys, values, boxes, lookup, slide)


def attend_back_kernel(
    q_ref,
    k_ref,
    v_ref,
    g_ref,
    box_ref,
    flip_ref,
    prob_ref,
    grad_ref,
    slide_sum_ref,
    box_sum_ref,
    slide_acc,
    box_acc,
):
    page = pl.program_id(0)

    @pl.when(page == 0)
    def _():
        slide_acc[...] = jnp.zeros_like(slide_acc)
        box_acc[...] = jnp.zeros_like(box_acc)

    boxes = box_ref[...]
    flipped = flip_ref[...]
    width = HEADS * HEAD_DIM
    for pair in range(PAIRS):
        at = slice(pair * NB, (pair + 1) * NB)
        prob = prob_ref[0, pair]
        pulled = split_heads(g_ref[:, at])
        d_prob = dot(v_ref[:, at], pulled, NT)
        prob_full = prob.astype(F32)
        inner = jnp.sum(prob_full * d_prob, axis=0, keepdims=True)
        d_logit = (prob_full * (d_prob - inner)).astype(BF)
        slide_acc[pair] += d_logit.astype(F32)
        offered = jnp.concatenate([k_ref[:, at], boxes], axis=1)
        back = dot(d_logit, offered, TN)
        scale = HEAD_DIM ** (-0.5)
        grad_ref[:, at] = (join_heads(back) * scale).astype(BF)
        grad_ref[:, width + pair * NB : width + (pair + 1) * NB] = dot(
            d_logit, split_heads(q_ref[:, at])
        ).astype(BF)
        grad_ref[:, 2 * width + pair * NB : 2 * width + (pair + 1) * NB] = dot(
            prob, pulled
        ).astype(BF)
        boxed = back[:, NB:].astype(BF)
        boxed = jnp.concatenate([boxed[:PAGE], boxed[PAGE:]], axis=1)
        box_acc[:, 2 * pair * NB : 2 * (pair + 1) * NB] += dot(flipped, boxed)

    @pl.when(page == PAGES - 1)
    def _():
        row = lax.broadcasted_iota(jnp.int32, (NB, NB), 0)
        lane = lax.broadcasted_iota(jnp.int32, (NB, NB), 1)
        mirror = (row + lane == NB - 1).astype(F32)
        same = (row < 64) == (lane >= 64)
        for head in range(HEADS):
            half = (head % 2) * PAGE
            block = slide_acc[head // 2, :, half : half + PAGE]
            block = lax.dot_general(
                mirror,
                block,
                (((1,), (0,)), ((), ())),
                precision=lax.Precision.HIGHEST,
                preferred_element_type=F32,
            )
            block = jnp.concatenate([block, jnp.zeros_like(block)], axis=1)
            slid = pltpu.roll(block, 0, 1, stride=1, stride_axis=0)
            slide_sum_ref[head : head + 1, :] = jnp.sum(slid, axis=0, keepdims=True)
            block = jnp.where(same, box_acc[:, head * NB : (head + 1) * NB], 0.0)
            slid = pltpu.roll(block, 0, 1, stride=1, stride_axis=0)
            box_sum_ref[1, head : head + 1, :] = jnp.sum(slid[:64], axis=0, keepdims=True)
            box_sum_ref[0, head : head + 1, :] = jnp.sum(slid[64:], axis=0, keepdims=True)


def attend_back(queries, keys, values, d_context, boxes, flipped, prob):
    width = HEADS * HEAD_DIM
    wide = pl.BlockSpec((PAGE, width), lambda i: (i, 0))
    return pl.pallas_call(
        attend_back_kernel,
        grid=(PAGES,),
        in_specs=[
            wide,
            wide,
            wide,
            wide,
            pl.BlockSpec((PAGE, NB), lambda i: (i, 0)),
            pl.BlockSpec((NB, PAGE), lambda i: (0, i)),
            pl.BlockSpec((1, PAIRS, PAGE, 2 * PAGE), lambda i: (i, 0, 0, 0)),
        ],
        out_specs=(
            pl.BlockSpec((PAGE, 3 * width), lambda i: (i, 0)),
            pl.BlockSpec((HEADS, 2 * PAGE), lambda i: (0, 0)),
            pl.BlockSpec((2, HEADS, NB), lambda i: (0, 0, 0)),
        ),
        out_shape=(
            jax.ShapeDtypeStruct((PAGES * PAGE, 3 * width), BF),
            jax.ShapeDtypeStruct((HEADS, 2 * PAGE), F32),
            jax.ShapeDtypeStruct((2, HEADS, NB), F32),
        ),
        scratch_shapes=[
            pltpu.VMEM((PAIRS, PAGE, 2 * PAGE), F32),
            pltpu.VMEM((NB, HEADS * NB), F32),
        ],
        compiler_params=pltpu.CompilerParams(vmem_limit_bytes=VMEM_LIMIT),
        cost_estimate=pl.CostEstimate(
            flops=10 * 10**9, bytes_accessed=20 * 2**20, transcendentals=0
        ),
    )(queries, keys, values, d_context, boxes, flipped, prob)


def fold_sums(slide_sum, box_sum):
    spot = np.zeros((2 * PAGE, NB), np.float32)
    for c in range(2 * PAGE - 1):
        spot[c, min(max(PAGE - 1 - c, -64), 63) + 64] = 1.0
    position = lax.dot_general(
        slide_sum,
        jnp.asarray(spot),
        (((1,), (0,)), ((), ())),
        precision=lax.Precision.HIGHEST,
        preferred_element_type=F32,
    )
    box = jnp.roll(box_sum, 65, axis=2)
    return jnp.concatenate([position[None], box], axis=0).transpose(0, 2, 1)


def norm_parts(values):
    center = jnp.mean(values, axis=-1, keepdims=True)
    centered = values - center
    spread = lax.rsqrt(jnp.mean(centered * centered, axis=-1, keepdims=True) + EPSILON)
    return centered * spread, spread


def norm_back(normed, spread, pulled):
    level = jnp.mean(pulled, axis=-1, keepdims=True)
    slope = jnp.mean(pulled * normed, axis=-1, keepdims=True)
    return spread * (pulled - level - normed * slope)


def on_device(line, *args):
    (
        hidden_in,
        cotangent,
        segment_ids,
        box_left,
        box_top,
        query_weight,
        query_bias,
        key_weight,
        value_weight,
        value_bias,
        output_weight,
        output_bias,
        first_gain,
        first_shift,
        inner_weight,
        inner_bias,
        outer_weight,
        outer_bias,
        second_gain,
        second_shift,
        bucket_table,
    ) = args
    row_count, slot_count = segment_ids.shape
    width = hidden_in.shape[1]
    vectors = (
        query_bias,
        value_bias,
        output_bias,
        first_gain,
        first_shift,
        inner_bias,
        outer_bias,
        second_gain,
        second_shift,
        bucket_table,
    )
    cuts = np.cumsum([0] + [item.shape[0] for item in vectors])
    small = jnp.concatenate(vectors)
    in_shard = jnp.concatenate([query_weight, key_weight, value_weight], axis=0)
    if line:
        me = lax.axis_index("fsdp")
        order = block_order(me)
        put = (order[None, :] == jnp.arange(8)[:, None]).astype(F32)
        small_all = dot(
            put.astype(BF), jnp.stack(gather_blocks(small.reshape(-1, 128))).reshape(8, -1)
        )
        in_all = place(order, gather_blocks(in_shard), 3)
        output_all = place(order, gather_blocks(output_weight))
        inner_all = place(order, gather_blocks(inner_weight))
        outer_all = place(order, gather_blocks(outer_weight))
    else:
        gather = partial(lax.all_gather, axis_name="fsdp", axis=0)
        small_all = gather(small).astype(F32)
        in_all = gather(in_shard).reshape(-1, 3, query_weight.shape[0], width)
        in_all = in_all.transpose(0, 2, 1, 3).reshape(width, 3 * width)
        output_all = gather(output_weight, tiled=True)
        inner_all = gather(inner_weight, tiled=True)
        outer_all = gather(outer_weight, tiled=True)
    fulls = [
        small_all[:, cuts[i] : cuts[i + 1]].reshape(-1) for i in range(len(vectors))
    ]
    (q_bias, v_bias, o_bias, gain1, shift1, i_bias, u_bias, gain2, shift2, table) = fulls

    slot = lax.iota(jnp.int32, slot_count)
    pages = lax.iota(jnp.int32, PAGES)
    member = segment_ids[:, None, :] == pages[None, :, None]
    lengths = jnp.sum(member, axis=2, dtype=jnp.int32)
    starts = jnp.sum(
        segment_ids[:, None, :] < pages[None, :, None], axis=2, dtype=jnp.int32
    )
    start_of = jnp.sum(jnp.where(member, starts[:, :, None], 0), axis=1)
    target = segment_ids * PAGE + slot[None, :] - start_of
    padded = lax.iota(jnp.int32, PAGES * PAGE)
    lookup, slide = make_tables(table.reshape(3, NB, HEADS).astype(BF))

    in_bias = jnp.concatenate([q_bias, jnp.zeros_like(q_bias), v_bias])
    rows = []
    for r in range(row_count):
        row = slice(r * slot_count, (r + 1) * slot_count)
        spread = (padded[:, None] == target[r][None, :]).astype(BF)
        coords = lax.iota(jnp.int32, 64)
        marks = jnp.concatenate(
            [box_left[r][:, None] == coords[None], box_top[r][:, None] == coords[None]], axis=1
        ).astype(BF)
        boxes = dot(spread, marks).astype(BF)
        flipped = dot(marks[:, ::-1], spread, (((0,), (1,)), ((), ()))).astype(BF)
        hidden = dot(spread, hidden_in[row]).astype(BF)
        mixed = dot(hidden, in_all) + in_bias
        queries = (mixed[:, :width] * HEAD_DIM ** (-0.5)).astype(BF)
        keys = mixed[:, width : 2 * width].astype(BF)
        values = mixed[:, 2 * width :].astype(BF)
        context, prob = attend(lengths[r], queries, keys, values, boxes, lookup, slide)
        context = dot(spread, context, TN).astype(BF)
        rows.append((spread, boxes, flipped, hidden, queries, keys, values, context, prob))
    context = jnp.concatenate([item[7] for item in rows], axis=0)

    attn_out = dot(context, output_all) + o_bias
    normed1, spread1 = norm_parts(hidden_in.astype(F32) + attn_out)
    first_out = normed1 * gain1 + shift1
    first_low = first_out.astype(BF)
    inner = dot(first_low, inner_all) + i_bias
    share = 0.5 * (1.0 + lax.erf(inner * np.float32(0.5**0.5)))
    active = (inner * share).astype(BF)
    steep = share + inner * jnp.exp(-0.5 * inner * inner) * np.float32((2 * np.pi) ** -0.5)
    steep = steep.astype(BF)
    outer = dot(active, outer_all) + u_bias
    normed2, spread2 = norm_parts(first_out + outer)
    layer_out = (normed2 * gain2 + shift2).astype(BF)

    upstream = cotangent.astype(F32)
    second_gain_grad = jnp.sum(upstream * normed2, axis=0)
    second_shift_grad = jnp.sum(upstream, axis=0)
    d_second = norm_back(normed2, spread2, upstream * gain2)
    d_outer = d_second.astype(BF)
    outer_bias_grad = jnp.sum(d_outer, axis=0, dtype=F32)
    outer_grad = dot(active, d_outer, TN).astype(BF)
    d_inner = (dot(d_outer, outer_all, NT) * steep).astype(BF)
    inner_bias_grad = jnp.sum(d_inner, axis=0, dtype=F32)
    inner_grad = dot(first_low, d_inner, TN).astype(BF)
    d_first = d_second + dot(d_inner, inner_all, NT)
    first_gain_grad = jnp.sum(d_first * normed1, axis=0)
    first_shift_grad = jnp.sum(d_first, axis=0)
    d_summed = norm_back(normed1, spread1, d_first * gain1)
    d_attn = d_summed.astype(BF)
    output_bias_grad = jnp.sum(d_attn, axis=0, dtype=F32)
    output_grad = dot(context, d_attn, TN).astype(BF)
    d_context = dot(d_attn, output_all, NT).astype(BF)

    pulled, in_grad, slide_sum, box_sum, in_bias_grad = [], 0.0, 0.0, 0.0, 0.0
    for r in range(row_count):
        row = slice(r * slot_count, (r + 1) * slot_count)
        spread, boxes, flipped, hidden, queries, keys, values, _, prob = rows[r]
        d_padded = dot(spread, d_context[row]).astype(BF)
        d_mixed, slide_part, box_part = attend_back(
            queries, keys, values, d_padded, boxes, flipped, prob
        )
        in_grad = in_grad + dot(hidden, d_mixed, TN)
        in_bias_grad = in_bias_grad + jnp.sum(d_mixed, axis=0, dtype=F32)
        slide_sum, box_sum = slide_sum + slide_part, box_sum + box_part
        back = dot(d_mixed, in_all, NT).astype(BF)
        pulled.append(dot(spread, back, TN))
    in_grad = in_grad.astype(BF)
    input_grad = d_summed + jnp.concatenate(pulled, axis=0)
    table_grad = fold_sums(slide_sum, box_sum).reshape(-1)

    grads = (
        in_bias_grad[:width],
        in_bias_grad[2 * width :],
        output_bias_grad,
        first_gain_grad,
        first_shift_grad,
        inner_bias_grad,
        outer_bias_grad,
        second_gain_grad,
        second_shift_grad,
        table_grad,
    )
    small_grad = jnp.concatenate(
        [item.reshape(small_all.shape[0], -1) for item in grads], axis=1
    )
    if line:
        picked = jnp.einsum(
            "bk,bn->kn", put, small_grad, precision=lax.Precision.HIGHEST
        ).reshape(8, -1, 128)
        outer_own = sum_line(scatter_blocks(*pick(order, outer_grad)))
        inner_own = sum_line(scatter_blocks(*pick(order, inner_grad)))
        output_own = sum_line(scatter_blocks(*pick(order, output_grad)))
        in_own = sum_line(scatter_blocks(*pick(order, in_grad)))
        small_own = sum_line_small(scatter_blocks(picked[:4], picked[4:])).reshape(-1)
    else:

        def reduce(value):
            value = lax.psum_scatter(value, "fsdp", scatter_dimension=0, tiled=True)
            return lax.psum(value, "dp")

        outer_own = reduce(outer_grad)
        inner_own = reduce(inner_grad)
        output_own = reduce(output_grad)
        in_own = reduce(in_grad)
        small_own = reduce(small_grad).reshape(-1)
    owned = [small_own[cuts[i] : cuts[i + 1]] for i in range(len(vectors))]
    in_own = in_own.astype(F32)
    return (
        layer_out,
        input_grad,
        in_own[:, :width],
        owned[0],
        in_own[:, width : 2 * width],
        in_own[:, 2 * width :],
        owned[1],
        output_own.astype(F32),
        owned[2],
        owned[3],
        owned[4],
        inner_own.astype(F32),
        owned[5],
        outer_own.astype(F32),
        owned[6],
        owned[7],
        owned[8],
        owned[9],
    )


def solution(mesh):
    line = mesh.shape["fsdp"] == 8 and mesh.shape["dp"] == 4
    both, across, flat = P(("fsdp", "dp"), None), P("fsdp", None), P("fsdp")
    return jax.shard_map(
        partial(on_device, line),
        mesh=mesh,
        in_specs=(both,) * 5
        + (across, flat, across, across, flat, across, flat, flat, flat)
        + (across, flat, across, flat, flat, flat, flat),
        out_specs=(both, both)
        + (across, flat, across, across, flat, across, flat, flat, flat)
        + (across, flat, across, flat, flat, flat, flat),
        check_vma=False,
    )
```

time: 1370 us -> 2040 us (1.49)
  Pallas kernels: 0 us -> 1600 us
  matrix products: 720 us -> 125 us
  waiting for transfers between devices: 370 us -> 86 us
  starting transfers between devices: 0.52 us -> 158 us
  blocking collectives: 122 us -> 0 us
  local copies, waits for them, and re-layouts: 70.8 us -> 25 us
  other arithmetic: 60.9 us -> 35.2 us
    pallas_call x0 -> x11, Pallas kernels: none -> 1600 us  [the longest x4 770 us: place(): pl.pallas_call(partial(place_kernel, parts), out_shape=jax.ShapeDtypeStru...]
    dot_general x40 -> x20, matrix products: 720 us -> 125 us  [the longest x17 123 us: dot(): lax.dot_general(left_side, right_side, dims, preferred_element_type=F32)]
    reduce_scatter x6 -> x0, waiting for transfers between devices: 366 us -> none  [the longest x1 118 us: on_device(): lax.psum_scatter(inner_weight_grad, 'fsdp', scatter_dimension=0, tiled=True)]
    ppermute x0 -> x100, starting transfers between devices: none -> 158 us  [the longest x12 67.1 us: sum_line(): up = lax.ppermute(up, 'dp', [(i, i + 1) for i in range(t)])]
    ppermute x0 -> x100, waiting for transfers between devices: none -> 86 us  [the longest x50 66.5 us: hop(): return lax.ppermute(value, 'fsdp', pairs)]
    all_gather x10 -> x0, blocking collectives: 85.6 us -> none  [the longest x1 10.2 us: on_device(): lax.all_gather(outer_bias, 'fsdp', axis=0, tiled=True)]
    convert_element_type x29 -> x6, other arithmetic: 40 us -> 4.8 us  [the longest x1 1.57 us: on_device(): outer_own.astype(F32)]
    unnamed x1 -> x0, blocking collectives: 24.1 us -> none
  transfers between devices with their start and end apart: 13 -> 100, of which waited for: 5 -> 17; matrix products, arithmetic and copies ran while one was open for 54% -> 6% of each run, Pallas kernels for 0% -> 62%
where the time goes in v1:
time: 2040 us; the launch traced here: 2030 us
  Pallas kernels  1600 us (78%)
  starting transfers between devices  158 us (8%)
  matrix products  125 us (6%)
  waiting for transfers between devices  86 us (4%)
  other arithmetic  35.2 us (2%)
  local copies, waits for them, and re-layouts  25 us (1%)
    pallas_call x4, Pallas kernels, place(): pl.pallas_call(partial(place_kernel, parts), out_shape=jax.ShapeDtypeStru...  770 us
    pallas_call x4, Pallas kernels, pick(): pl.pallas_call(pick_kernel, out_shape=(shape, shape), in_specs=[pl.BlockS...  770 us
    dot_general x17, matrix products, dot(): lax.dot_general(left_side, right_side, dims, preferred_element_type=F32)  123 us
    ppermute x12, starting transfers between devices, sum_line(): up = lax.ppermute(up, 'dp', [(i, i + 1) for i in range(t)])  67.1 us
    ppermute x50, waiting for transfers between devices, hop(): return lax.ppermute(value, 'fsdp', pairs)  66.5 us
  transfers between devices with their start and end apart: 100, of which 17 were waited for; matrix products, arithmetic and copies ran while one was open for 6% of the time, Pallas kernels for 62%

profile of v1, /device:TPU:0, one launch (start us, length us, event | category | flops | bytes accessed | tf_op | source)
XLA Modules:
  0.0 2030.4 jit_solution(13134043317901456006)
XLA Ops:
  49.4 11.1 collective-permute-done.2.refs_3_
  66.9 65.4 %shard_map.379 = bf16[1024,1024]{1,0:T(8,128)(2,1)} custom-call(s32[8]{0:T(128)} %copy-done.21, bf16[128,1024]{1,0:T(8,128)(2,1)} %refs_0_.3, bf16[128,1024]{1,0:T(8,128)(2,1)} %copy-done.15, bf16[128,1024]{1,0:T(8,128)(2,1)} %collective-permute-done.15.refs_2_, bf16[128,1024]{1,0:T(8,128)(2,1)} %collective-permute-done.16.refs_3_, ...), custom_call_target="tpu_custom_call" | custom-call | bytes 4194304 | tf_op jit(solution)/shard_map/pallas_call | solution.py:126
  136.6 192.6 %shard_map.376 = bf16[1024,3072]{1,0:T(8,128)(2,1)} custom-call(s32[8]{0:T(128)} %copy-done.21, bf16[384,1024]{1,0:T(8,128)(2,1)} %copy-done.11, bf16[384,1024]{1,0:T(8,128)(2,1)} %copy-done.12, bf16[384,1024]{1,0:T(8,128)(2,1)} %copy-done.13, bf16[384,1024]{1,0:T(8,128)(2,1)} %collective-permute-done.2.refs_3_, ...), custom_call_target="tpu_custom_call" | custom-call | bytes 12582912 | tf_op jit(solution)/shard_map/pallas_call | solution.py:126
  329.2 9.0 fusion.76
  341.3 33.6 %shard_map.378 = (bf16[1024,1024]{1,0:T(8,128)(2,1)S(1)}, bf16[8,8,128,256]{3,2,1,0:T(8,128)(2,1)}) custom-call(s32[8]{0:T(128)S(1)} %get-tuple-element.57.length_ref, bf16[1024,1024]{1,0:T(8,128)(2,1)S(1)} %fusion.5.q_ref, bf16[1024,1024]{1,0:T(8,128)(2,1)} %get-tuple-element.69.k_ref, bf16[1024,1024]{1,0:T(8,128)(2,1)} %get-tuple-element.68.v_ref, ...), custom_call_target="tpu_custom_call" | custom-call | flops 6000000000 | bytes 14680064 | tf_op jit(solution)/shard_map/pallas_call | solution.py:247
  381.9 10.2 collective-permute-done.30.refs_3_
  392.1 256.0 %shard_map.380 = bf16[1024,4096]{1,0:T(8,128)(2,1)} custom-call(s32[8]{0:T(128)} %copy-done.21, bf16[128,4096]{1,0:T(8,128)(2,1)} %refs_0_.4, bf16[128,4096]{1,0:T(8,128)(2,1)} %collective-permute-done.21.refs_1_, bf16[128,4096]{1,0:T(8,128)(2,1)} %collective-permute-done.22.refs_2_, bf16[128,4096]{1,0:T(8,128)(2,1)} %collective-permute-done.23.refs_3_, ...), custom_call_target="tpu_custom_call" | custom-call | bytes 16777216 | tf_op jit(solution)/shard_map/pallas_call | solution.py:126
  648.0 11.8 multiply_convert_fusion.1
  659.9 256.0 %shard_map.381 = bf16[4096,1024]{1,0:T(8,128)(2,1)} custom-call(s32[8]{0:T(128)} %copy-done.21, bf16[512,1024]{1,0:T(8,128)(2,1)} %refs_0_.5, bf16[512,1024]{1,0:T(8,128)(2,1)} %collective-permute-done.28.refs_1_, bf16[512,1024]{1,0:T(8,128)(2,1)} %collective-permute-done.29.refs_2_, bf16[512,1024]{1,0:T(8,128)(2,1)} %collective-permute-done.30.refs_3_, ...), custom_call_target="tpu_custom_call" | custom-call | bytes 16777216 | tf_op jit(solution)/shard_map/pallas_call | solution.py:126
  915.8 10.3 fusion.78
  930.4 13.8 convert_reduce_fusion.1
  966.6 22.9 %shard_map.382 = (bf16[1024,3072]{1,0:T(8,128)(2,1)}, f32[16,256]{1,0:T(8,128)S(1)}, f32[2,16,128]{2,1,0:T(8,128)S(1)}) custom-call(bf16[1024,1024]{1,0:T(8,128)(2,1)S(1)} %fusion.5.q_ref, bf16[1024,1024]{1,0:T(8,128)(2,1)S(1)} %copy-done, bf16[1024,1024]{1,0:T(8,128)(2,1)} %get-tuple-element.68.v_ref, bf16[1024,1024]{1,0:T(8,128)(2,1)} %fusion.22.g_ref, ...), custom_call_target="tpu_custom_call" | custom-call | flops 10000000000 | bytes 20971520 | tf_op jit(solution)/shard_map/pallas_call | solution.py:351
  993.9 65.4 %shard_map.384 = (bf16[4,128,1024]{2,1,0:T(8,128)(2,1)}, bf16[4,128,1024]{2,1,0:T(8,128)(2,1)}) custom-call(s32[8]{0:T(128)} %copy-done.21, bf16[1024,1024]{1,0:T(8,128)(2,1)} %convolution_convert_fusion.3.grad_ref), custom_call_target="tpu_custom_call" | custom-call | bytes 4194304 | tf_op jit(solution)/shard_map/pallas_call | solution.py:159
  1065.7 11.3 convolution_convert_fusion.2.grad_ref
  1077.0 192.4 %shard_map.383 = (bf16[4,128,3072]{2,1,0:T(8,128)(2,1)}, bf16[4,128,3072]{2,1,0:T(8,128)(2,1)}) custom-call(s32[8]{0:T(128)} %copy-done.21, bf16[1024,3072]{1,0:T(8,128)(2,1)} %convolution_convert_fusion.2.grad_ref), custom_call_target="tpu_custom_call" | custom-call | bytes 12582912 | tf_op jit(solution)/shard_map/pallas_call | solution.py:159
  1271.8 14.5 fusion.23
  1292.6 11.6 convolution_convert_fusion.grad_ref
  1304.2 256.0 %shard_map.385 = (bf16[4,128,4096]{2,1,0:T(8,128)(2,1)}, bf16[4,128,4096]{2,1,0:T(8,128)(2,1)}) custom-call(s32[8]{0:T(128)} %copy-done.21, bf16[1024,4096]{1,0:T(8,128)(2,1)} %convolution_convert_fusion.grad_ref), custom_call_target="tpu_custom_call" | custom-call | bytes 16777216 | tf_op jit(solution)/shard_map/pallas_call | solution.py:159
  1572.8 11.6 convolution_convert_fusion.1.grad_ref
  1584.5 256.0 %shard_map.386 = (bf16[4,512,1024]{2,1,0:T(8,128)(2,1)}, bf16[4,512,1024]{2,1,0:T(8,128)(2,1)}) custom-call(s32[8]{0:T(128)} %copy-done.21, bf16[4096,1024]{1,0:T(8,128)(2,1)} %convolution_convert_fusion.1.grad_ref), custom_call_target="tpu_custom_call" | custom-call | bytes 16777216 | tf_op jit(solution)/shard_map/pallas_call | solution.py:159
  1870.2 12.8 collective-permute-done.37
  1901.4 13.0 collective-permute-start.40
  1925.1 20.0 collective-permute-done.86
  1949.6 9.2 collective-permute-start.73
  (416 shorter events, 261.4 us)
Async XLA Ops:
  47.1 85.8 %collective-permute-start.21 = (bf16[128,4096]{1,0:T(8,128)(2,1)}, bf16[128,4096]{1,0:T(8,128)(2,1)}, u32[]{:S(2)}, u32[]{:S(2)}) collective-permute-start(bf16[128,4096]{1,0:T(8,128)(2,1)} %refs_0_.4), channel_id=1, source_target_pairs={{0,16},{4,12},{8,24},{12,4},{16,0},{20,28},{24,8},{28,20},{1,17},{... | collective-permute-start | bytes 3145736 | tf_op jit(solution)/shard_map/ppermute | solution.py:47
  47.8 84.5 %collective-permute-start.3 = (bf16[384,1024]{1,0:T(8,128)(2,1)S(1)}, bf16[384,1024]{1,0:T(8,128)(2,1)}, u32[]{:S(2)}, u32[]{:S(2)}) collective-permute-start(bf16[384,1024]{1,0:T(8,128)(2,1)S(1)} %constant_dynamic-update-slice_fusion.refs_0_), channel_id=1, source_target_pairs={{0,4},{4,0},{8,12},{12,8},{16,20},{20,16},{24,28},{28,24},{1,5},{5... | collective-permute-start | bytes 2359304 | tf_op jit(solution)/shard_map/ppermute | solution.py:47
  48.9 84.2 %collective-permute-start.4 = (bf16[384,1024]{1,0:T(8,128)(2,1)S(1)}, bf16[384,1024]{1,0:T(8,128)(2,1)}, u32[]{:S(2)}, u32[]{:S(2)}) collective-permute-start(bf16[384,1024]{1,0:T(8,128)(2,1)S(1)} %collective-permute-done.refs_1_), channel_id=1, source_target_pairs={{0,4},{4,0},{8,12},{12,8},{16,20},{20,16},{24,28},{28,24},{1,5},{5... | collective-permute-start | bytes 2359304 | tf_op jit(solution)/shard_map/ppermute | solution.py:47
  49.0 85.6 %collective-permute-start.5 = (bf16[384,1024]{1,0:T(8,128)(2,1)S(1)}, bf16[384,1024]{1,0:T(8,128)(2,1)}, u32[]{:S(2)}, u32[]{:S(2)}) collective-permute-start(bf16[384,1024]{1,0:T(8,128)(2,1)S(1)} %collective-permute-done.1.refs_2_), channel_id=1, source_target_pairs={{0,4},{4,0},{8,12},{12,8},{16,20},{20,16},{24,28},{28,24},{1,5},{5... | collective-permute-start | bytes 2359304 | tf_op jit(solution)/shard_map/ppermute | solution.py:47
  132.3 244.1 %collective-permute-start.22 = (bf16[128,4096]{1,0:T(8,128)(2,1)}, bf16[128,4096]{1,0:T(8,128)(2,1)}, u32[]{:S(2)}, u32[]{:S(2)}) collective-permute-start(bf16[128,4096]{1,0:T(8,128)(2,1)} %refs_0_.4), channel_id=1, source_target_pairs={{0,8},{4,20},{8,0},{12,28},{16,24},{20,4},{24,16},{28,12},{1,9},{5... | collective-permute-start | bytes 3145736 | tf_op jit(solution)/shard_map/ppermute | solution.py:47
  133.0 243.5 %collective-permute-start.24 = (bf16[128,4096]{1,0:T(8,128)(2,1)}, bf16[128,4096]{1,0:T(8,128)(2,1)}, u32[]{:S(2)}, u32[]{:S(2)}) collective-permute-start(bf16[128,4096]{1,0:T(8,128)(2,1)} %refs_0_.4), channel_id=1, source_target_pairs={{0,4},{4,0},{8,12},{12,8},{16,20},{20,16},{24,28},{28,24},{1,5},{5... | collective-permute-start | bytes 3145736 | tf_op jit(solution)/shard_map/ppermute | solution.py:47
  133.1 243.9 %collective-permute-start.28 = (bf16[512,1024]{1,0:T(8,128)(2,1)}, bf16[512,1024]{1,0:T(8,128)(2,1)}, u32[]{:S(2)}, u32[]{:S(2)}) collective-permute-start(bf16[512,1024]{1,0:T(8,128)(2,1)} %refs_0_.5), channel_id=1, source_target_pairs={{0,16},{4,12},{8,24},{12,4},{16,0},{20,28},{24,8},{28,20},{1,17},{... | collective-permute-start | bytes 3145736 | tf_op jit(solution)/shard_map/ppermute | solution.py:47
  134.6 246.2 %collective-permute-start.29 = (bf16[512,1024]{1,0:T(8,128)(2,1)}, bf16[512,1024]{1,0:T(8,128)(2,1)}, u32[]{:S(2)}, u32[]{:S(2)}) collective-permute-start(bf16[512,1024]{1,0:T(8,128)(2,1)} %refs_0_.5), channel_id=1, source_target_pairs={{0,8},{4,20},{8,0},{12,28},{16,24},{20,4},{24,16},{28,12},{1,9},{5... | collective-permute-start | bytes 3145736 | tf_op jit(solution)/shard_map/ppermute | solution.py:47
  135.2 242.3 %collective-permute-start.23 = (bf16[128,4096]{1,0:T(8,128)(2,1)}, bf16[128,4096]{1,0:T(8,128)(2,1)}, u32[]{:S(2)}, u32[]{:S(2)}) collective-permute-start(bf16[128,4096]{1,0:T(8,128)(2,1)} %collective-permute-done.21.refs_1_), channel_id=1, source_target_pairs={{0,8},{4,20},{8,0},{12,28},{16,24},{20,4},{24,16},{28,12},{1,9},{5... | collective-permute-start | bytes 3145736 | tf_op jit(solution)/shard_map/ppermute | solution.py:47
  380.8 279.0 %collective-permute-start.31 = (bf16[512,1024]{1,0:T(8,128)(2,1)}, bf16[512,1024]{1,0:T(8,128)(2,1)}, u32[]{:S(2)}, u32[]{:S(2)}) collective-permute-start(bf16[512,1024]{1,0:T(8,128)(2,1)} %refs_0_.5), channel_id=1, source_target_pairs={{0,4},{4,0},{8,12},{12,8},{16,20},{20,16},{24,28},{28,24},{1,5},{5... | collective-permute-start | bytes 3145736 | tf_op jit(solution)/shard_map/ppermute | solution.py:47
  381.3 278.5 %collective-permute-start.32 = (bf16[512,1024]{1,0:T(8,128)(2,1)}, bf16[512,1024]{1,0:T(8,128)(2,1)}, u32[]{:S(2)}, u32[]{:S(2)}) collective-permute-start(bf16[512,1024]{1,0:T(8,128)(2,1)} %collective-permute-done.28.refs_1_), channel_id=1, source_target_pairs={{0,4},{4,0},{8,12},{12,8},{16,20},{20,16},{24,28},{28,24},{1,5},{5... | collective-permute-start | bytes 3145736 | tf_op jit(solution)/shard_map/ppermute | solution.py:47
  381.4 278.4 %collective-permute-start.33 = (bf16[512,1024]{1,0:T(8,128)(2,1)}, bf16[512,1024]{1,0:T(8,128)(2,1)}, u32[]{:S(2)}, u32[]{:S(2)}) collective-permute-start(bf16[512,1024]{1,0:T(8,128)(2,1)} %collective-permute-done.29.refs_2_), channel_id=1, source_target_pairs={{0,4},{4,0},{8,12},{12,8},{16,20},{20,16},{24,28},{28,24},{1,5},{5... | collective-permute-start | bytes 3145736 | tf_op jit(solution)/shard_map/ppermute | solution.py:47
  392.0 267.8 %collective-permute-start.34 = (bf16[512,1024]{1,0:T(8,128)(2,1)}, bf16[512,1024]{1,0:T(8,128)(2,1)}, u32[]{:S(2)}, u32[]{:S(2)}) collective-permute-start(bf16[512,1024]{1,0:T(8,128)(2,1)} %collective-permute-done.30.refs_3_), channel_id=1, source_target_pairs={{0,4},{4,0},{8,12},{12,8},{16,20},{20,16},{24,28},{28,24},{1,5},{5... | collective-permute-start | bytes 3145736 | tf_op jit(solution)/shard_map/ppermute | solution.py:47
  1062.2 207.3 %collective-permute-start.51 = (f32[2,18,128]{2,1,0:T(8,128)S(1)}, f32[2,18,128]{2,1,0:T(8,128)S(1)}, u32[]{:S(2)}, u32[]{:S(2)}) collective-permute-start(f32[2,18,128]{2,1,0:T(8,128)S(1)} %get-tuple-element.127), channel_id=1, source_target_pairs={{0,8},{4,20},{8,0},{12,28},{16,24},{20,4},{24,16},{28,12},{1,9},{5... | collective-permute-start | bytes 55304 | tf_op jit(solution)/shard_map/ppermute | solution.py:47
  1064.2 206.0 %collective-permute-start.56 = (bf16[2,128,1024]{2,1,0:T(8,128)(2,1)S(1)}, bf16[2,128,1024]{2,1,0:T(8,128)(2,1)S(1)}, u32[]{:S(2)}, u32[]{:S(2)}) collective-permute-start(bf16[2,128,1024]{2,1,0:T(8,128)(2,1)S(1)} %get-tuple-element.72), channel_id=1, source_target_pairs={{0,8},{4,20},{8,0},{12,28},{16,24},{20,4},{24,16},{28,12},{1,9},{5... | collective-permute-start | bytes 1572872 | tf_op jit(solution)/shard_map/ppermute | solution.py:47
  1269.5 298.3 %collective-permute-start.35 = (bf16[4,128,3072]{2,1,0:T(8,128)(2,1)}, bf16[4,128,3072]{2,1,0:T(8,128)(2,1)}, u32[]{:S(2)}, u32[]{:S(2)}) collective-permute-start(bf16[4,128,3072]{2,1,0:T(8,128)(2,1)} %get-tuple-element.39), channel_id=1, source_target_pairs={{0,4},{4,0},{8,12},{12,8},{16,20},{20,16},{24,28},{28,24},{1,5},{5... | collective-permute-start | bytes 9437192 | tf_op jit(solution)/shard_map/ppermute | solution.py:47
  1287.0 273.2 %collective-permute-start.53 = (f32[18,128]{1,0:T(8,128)S(1)}, f32[18,128]{1,0:T(8,128)}, u32[]{:S(2)}, u32[]{:S(2)}) collective-permute-start(f32[18,128]{1,0:T(8,128)S(1)} %fusion.56), channel_id=1, source_target_pairs={{0,1},{1,0},{2,3},{3,2},{4,5},{5,4},{6,7},{7,6},{8,9},{9,8},{10,11... | collective-permute-start | bytes 27656 | tf_op jit(solution)/shard_map/ppermute | solution.py:99
  1289.6 272.9 %collective-permute-start.58 = (bf16[32,1024]{1,0:T(8,128)(2,1)S(1)}, bf16[32,1024]{1,0:T(8,128)(2,1)S(1)}, u32[]{:S(2)}, u32[]{:S(2)}) collective-permute-start(bf16[32,1024]{1,0:T(8,128)(2,1)S(1)} %get-tuple-element.114), channel_id=1, source_target_pairs={{0,1},{4,5},{8,9},{12,13},{16,17},{20,21},{24,25},{28,29}} | collective-permute-start | bytes 196616 | tf_op jit(solution)/shard_map/ppermute | solution.py:78
  1292.0 270.5 %collective-permute-start.61 = (bf16[32,1024]{1,0:T(8,128)(2,1)S(1)}, bf16[32,1024]{1,0:T(8,128)(2,1)S(1)}, u32[]{:S(2)}, u32[]{:S(2)}) collective-permute-start(bf16[32,1024]{1,0:T(8,128)(2,1)S(1)} %get-tuple-element.115), channel_id=1, source_target_pairs={{3,2},{7,6},{11,10},{15,14},{19,18},{23,22},{27,26},{31,30}} | collective-permute-start | bytes 196616 | tf_op jit(solution)/shard_map/ppermute | solution.py:79
  1560.2 305.6 %collective-permute-start.70 = (bf16[4,128,4096]{2,1,0:T(8,128)(2,1)}, bf16[4,128,4096]{2,1,0:T(8,128)(2,1)}, u32[]{:S(2)}, u32[]{:S(2)}) collective-permute-start(bf16[4,128,4096]{2,1,0:T(8,128)(2,1)} %get-tuple-element.45), channel_id=1, source_target_pairs={{0,4},{4,0},{8,12},{12,8},{16,20},{20,16},{24,28},{28,24},{1,5},{5... | collective-permute-start | bytes 12582920 | tf_op jit(solution)/shard_map/ppermute | solution.py:47
  1561.0 279.5 %collective-permute-start.54 = (f32[18,128]{1,0:T(8,128)S(1)}, f32[18,128]{1,0:T(8,128)S(1)}, u32[]{:S(2)}, u32[]{:S(2)}) collective-permute-start(f32[18,128]{1,0:T(8,128)S(1)} %add.402), channel_id=1, source_target_pairs={{0,2},{1,3},{2,0},{3,1},{4,6},{5,7},{6,4},{7,5},{8,10},{9,11},{10,... | collective-permute-start | bytes 27656 | tf_op jit(solution)/shard_map/ppermute | solution.py:100
  1562.5 278.0 %collective-permute-start.59 = (bf16[32,1024]{1,0:T(8,128)(2,1)S(1)}, bf16[32,1024]{1,0:T(8,128)(2,1)S(1)}, u32[]{:S(2)}, u32[]{:S(2)}) collective-permute-start(bf16[32,1024]{1,0:T(8,128)(2,1)S(1)} %get-tuple-element.112), channel_id=1, source_target_pairs={{0,1},{1,2},{4,5},{5,6},{8,9},{9,10},{12,13},{13,14},{16,17},{17,1... | collective-permute-start | bytes 196616 | tf_op jit(solution)/shard_map/ppermute | solution.py:78
  1567.1 273.5 %collective-permute-start.62 = (bf16[32,1024]{1,0:T(8,128)(2,1)S(1)}, bf16[32,1024]{1,0:T(8,128)(2,1)S(1)}, u32[]{:S(2)}, u32[]{:S(2)}) collective-permute-start(bf16[32,1024]{1,0:T(8,128)(2,1)S(1)} %get-tuple-element.113), channel_id=1, source_target_pairs={{3,2},{2,1},{7,6},{6,5},{11,10},{10,9},{15,14},{14,13},{19,18},{18... | collective-permute-start | bytes 196616 | tf_op jit(solution)/shard_map/ppermute | solution.py:79
  1572.2 291.1 %collective-permute-start.36 = (bf16[2,128,3072]{2,1,0:T(8,128)(2,1)}, bf16[2,128,3072]{2,1,0:T(8,128)(2,1)}, u32[]{:S(2)}, u32[]{:S(2)}) collective-permute-start(bf16[2,128,3072]{2,1,0:T(8,128)(2,1)} %get-tuple-element.67), channel_id=1, source_target_pairs={{0,8},{4,20},{8,0},{12,28},{16,24},{20,4},{24,16},{28,12},{1,9},{5... | collective-permute-start | bytes 4718600 | tf_op jit(solution)/shard_map/ppermute | solution.py:47
  (115 other events, 5282.6 us)
